TPU v7x, 256 devices: a whole 4x4x8 slice. The times are simulated.
256 devices in a mesh: cfg: 2 (over core), tok: 8 (over z), mlp: 16 (over x, y).
Axes of the slice: x: 4, y: 4, z: 8, core: 2. Of those that a mesh axis runs over, the one named last changes fastest.
Arguments:
- hidden: bfloat16 [2, 1536, 4, 3072], P('cfg', ('tok', 'mlp')), may hold values from -6 to 6
- latents: float32 [1536, 4, 64], P(('tok', 'mlp'), None, 'cfg'), may hold values from -6 to 6
- vec: float32 [2, 4, 3072], P('cfg'), may hold values from -9 to 9
- slot_token: int32 [4, 1536], replicated, may hold values from 0 to 1535, each once within a row
- text_len: int32 [2, 4], P('cfg'), may hold values from 64 to 512, as said below
- step_index: int32 [1], replicated, may hold values from 0 to 27
- guidance: float32 [1], replicated, may hold values from 2 to 5
- w_mod: bfloat16 [3072, 15360], P(None, ('tok', 'mlp')), may hold values from -0.109375 to 0.109375
- w_qkv: bfloat16 [1, 3072, 3, 2048], P(None, 'cfg', None, 'mlp'), may hold values from -0.109375 to 0.109375
- w_mlp_in: bfloat16 [1, 3072, 12288], P(None, 'cfg', 'mlp'), may hold values from -0.109375 to 0.109375
- qk_gain: float32 [1, 2, 128], replicated, may hold values from 1.5 to 2.5
- w_attn_out: bfloat16 [1, 2048, 3072], P(None, 'mlp', 'cfg'), may hold values from -0.125 to 0.125
- w_mlp_out: bfloat16 [1, 12288, 3072], P(None, 'mlp', 'cfg'), may hold values from -0.0546875 to 0.0546875
- w_final: bfloat16 [3072, 64], replicated, may hold values from -0.109375 to 0.109375
Outputs:
- velocity: float32 [1536, 4, 64], P(('tok', 'mlp'), None, 'cfg')
- latents_next: float32 [1536, 4, 64], P(('tok', 'mlp'), None, 'cfg')
- stream_out: bfloat16 [2, 1536, 4, 3072], P('cfg', ('tok', 'mlp'))
Inputs may be any that keep to these rules, and one draw needn't show every extreme that they name: `text_len`: real text tokens of each request; its other text slots are padding; exactly one request has all 512. `slot_token`: row p lists the token held by each slot of request p: text tokens are 0 to 511, image tokens follow row by row on the 32 x 32 grid.
All inputs are finite; a program needn't handle non-finite values.
Results may differ from a plain program's by a relative error of at most 0.018.
Values may be sent and summed in bfloat16 or wider, within the bound.
A program may use at most 128 MiB of HBM per device.

v0:
```python
import math
import jax
import jax.numpy as jnp
from jax import lax
from jax.sharding import PartitionSpec as P

LAYERS = 1
SIDE = 32
TXT = 512
STEPS = 28
EPSILON = 1e-06
ROPE_BASE = 10000.0
TIME_SHIFT = 3.0


def swapped(value, axis, apart):
    return lax.ppermute(value, axis, [(i, i ^ 1 << apart) for i in range(lax.axis_size(axis))])


def layer_norm(values):
    average = jnp.mean(values, axis=-1, keepdims=True)
    centred = values - average
    spread = jnp.mean(centred * centred, axis=-1, keepdims=True)
    return centred * lax.rsqrt(spread + EPSILON)


def rms_norm(values, gains):
    return values * lax.rsqrt(jnp.mean(values * values, axis=-1, keepdims=True) + EPSILON) * gains


def rope_table(tokens, head_size, text_count, side_count):
    pair_count = head_size // 2
    first_pairs = head_size // 16
    axis_pairs = (head_size - head_size // 8) // 4
    pair_index = jnp.arange(pair_count).astype(jnp.float32)
    in_rows = (pair_index >= first_pairs) & (pair_index < first_pairs + axis_pairs)
    in_cols = pair_index >= first_pairs + axis_pairs
    log_base = math.log(ROPE_BASE)
    freq_rows = jnp.where(
        in_rows, jnp.exp(-log_base * (pair_index - first_pairs) / axis_pairs), 0.0
    )
    freq_cols = jnp.where(
        in_cols, jnp.exp(-log_base * (pair_index - first_pairs - axis_pairs) / axis_pairs), 0.0
    )
    is_image = tokens >= text_count
    image_pos = jnp.where(is_image, tokens - text_count, 0)
    row_pos = (image_pos // side_count).astype(jnp.float32)
    col_pos = (image_pos % side_count).astype(jnp.float32)
    angles = row_pos[..., None] * freq_rows + col_pos[..., None] * freq_cols
    return (jnp.cos(angles), jnp.sin(angles))


def apply_rope(values, cosine, sine_table):
    even_part = values[..., 0::2]
    odd_part = values[..., 1::2]
    return jnp.concatenate(
        [even_part * cosine - odd_part * sine_table, even_part * sine_table + odd_part * cosine],
        axis=-1,
    )


def sigma_at(position, steps_total):
    remain = 1.0 - position / steps_total
    return TIME_SHIFT * remain / (1.0 + (TIME_SHIFT - 1.0) * remain)


def on_device(
    hidden,
    latents,
    vec,
    slot_token,
    text_len,
    step_index,
    guidance,
    w_mod,
    w_qkv,
    w_mlp_in,
    qk_gain,
    w_attn_out,
    w_mlp_out,
    w_final,
):
    rows_dev = hidden.shape[1]
    prompts = hidden.shape[2]
    model_width = hidden.shape[3]
    head_size = qk_gain.shape[-1]
    mlp_count = lax.axis_size("mlp")
    tile_rows = rows_dev * mlp_count
    tok_index = lax.axis_index("tok")
    mlp_index = lax.axis_index("mlp")
    half_index = lax.axis_index("cfg")
    first_half = half_index == 0
    stream = hidden[0]
    silu_vec = jax.nn.silu(vec[0]).astype(jnp.bfloat16)
    mod_part = jnp.dot(silu_vec, w_mod, preferred_element_type=jnp.float32)
    modulation = lax.all_gather(mod_part, ("tok", "mlp"), axis=1, tiled=True)
    key_valid = ((slot_token >= TXT) | (slot_token < text_len[0][:, None])).astype(jnp.float32)
    tile_tokens = lax.dynamic_slice_in_dim(slot_token, tok_index * tile_rows, tile_rows, 1).T
    cosine, sine_table = rope_table(tile_tokens, head_size, TXT, SIDE)
    shift_mod = modulation[:, 0:model_width]
    scale_mod = modulation[:, model_width : 2 * model_width]
    gate_mod = modulation[:, 2 * model_width : 3 * model_width]
    normed = (
        layer_norm(stream.astype(jnp.float32)) * (1.0 + scale_mod[None]) + shift_mod[None]
    ).astype(jnp.bfloat16)
    tile_input = lax.all_gather(normed, "mlp", axis=0, tiled=True)
    qkv_weight = w_qkv[0]
    unit_weight = w_mlp_in[0]
    qkv_cols = qkv_weight.shape[1] * qkv_weight.shape[2]
    pieces = (
        lax.all_gather(qkv_weight, "cfg", axis=0, tiled=True),
        lax.all_gather(unit_weight, "cfg", axis=0, tiled=True),
    )
    number = pieces[0].shape[0]
    qkv_piece = pieces[0].reshape(number, qkv_cols)
    qkv_pre = jnp.einsum("tpd,dk->tpk", tile_input, qkv_piece, preferred_element_type=jnp.float32)
    unit_pre = jnp.einsum("tpd,dk->tpk", tile_input, pieces[1], preferred_element_type=jnp.float32)
    heads_dev = qkv_weight.shape[2] // head_size
    projected = qkv_pre.reshape(tile_rows, prompts, 3, heads_dev, head_size)
    queries = apply_rope(
        rms_norm(projected[:, :, 0], qk_gain[0, 0]), cosine[:, :, None], sine_table[:, :, None]
    ).astype(jnp.bfloat16)
    keys_rot = apply_rope(
        rms_norm(projected[:, :, 1], qk_gain[0, 1]), cosine[:, :, None], sine_table[:, :, None]
    ).astype(jnp.bfloat16)
    values = projected[:, :, 2].astype(jnp.bfloat16)
    activation = jax.nn.gelu(unit_pre, approximate=True).astype(jnp.bfloat16)
    keys_piece = lax.all_gather(keys_rot, "tok", axis=0, tiled=True)
    values_piece = lax.all_gather(values, "tok", axis=0, tiled=True)
    scores = jnp.einsum(
        "sphe,tphe->phst", queries, keys_piece, preferred_element_type=jnp.float32
    ) / math.sqrt(head_size)
    softened = jnp.exp(scores) * key_valid[:, None, None, :]
    numerator = jnp.einsum(
        "phst,tphe->sphe",
        softened.astype(jnp.bfloat16),
        values_piece,
        preferred_element_type=jnp.float32,
    )
    numerator, denominator = (numerator, jnp.sum(softened, axis=-1))
    attended = (numerator / jnp.transpose(denominator, (2, 0, 1))[..., None]).astype(jnp.bfloat16)
    attended = attended.reshape(tile_rows, prompts, heads_dev * head_size)
    out_attn = lax.all_gather(w_attn_out[0], "cfg", axis=1, tiled=True)
    out_units = lax.all_gather(w_mlp_out[0], "cfg", axis=1, tiled=True)
    branch_out = lax.psum_scatter(
        (
            jnp.einsum("tpk,kd->tpd", attended, out_attn, preferred_element_type=jnp.float32)
            + jnp.einsum("tpk,kd->tpd", activation, out_units, preferred_element_type=jnp.float32)
        ).astype(jnp.bfloat16),
        "mlp",
        scatter_dimension=0,
        tiled=True,
    ).astype(jnp.float32)
    stream = (stream.astype(jnp.float32) + gate_mod[None] * branch_out).astype(jnp.bfloat16)
    final_lo = 3 * LAYERS * model_width
    final_shift = modulation[:, final_lo : final_lo + model_width]
    final_scale = modulation[:, final_lo + model_width : final_lo + 2 * model_width]
    final_normed = (
        layer_norm(stream.astype(jnp.float32)) * (1.0 + final_scale[None]) + final_shift[None]
    ).astype(jnp.bfloat16)
    own_first = (tok_index * mlp_count + mlp_index) * rows_dev
    own_tokens = lax.dynamic_slice_in_dim(slot_token, own_first, rows_dev, 1).T
    half_velocity = jnp.einsum(
        "rpd,dc->rpc", final_normed, w_final, preferred_element_type=jnp.float32
    )
    half_velocity = jnp.where((own_tokens >= TXT)[:, :, None], half_velocity, 0.0)
    channel_half = latents.shape[2]
    own_part = lax.dynamic_slice_in_dim(half_velocity, half_index * channel_half, channel_half, 2)
    sent_part = lax.dynamic_slice_in_dim(
        half_velocity, (1 - half_index) * channel_half, channel_half, 2
    )
    partner = swapped(sent_part, "cfg", 0)
    cond_part = jnp.where(first_half, own_part, partner)
    uncond_part = jnp.where(first_half, partner, own_part)
    velocity = uncond_part + guidance[0] * (cond_part - uncond_part)
    current = step_index[0].astype(jnp.float32)
    step_size = sigma_at(current + 1.0, STEPS) - sigma_at(current, STEPS)
    return (velocity, latents + step_size * velocity, stream[None])


def solution(mesh):
    return jax.shard_map(
        on_device,
        mesh=mesh,
        in_specs=(
            P("cfg", ("tok", "mlp"), None, None),
            P(("tok", "mlp"), None, "cfg"),
            P("cfg", None, None),
            P(),
            P("cfg", None),
            P(),
            P(),
            P(None, ("tok", "mlp")),
            P(None, "cfg", None, "mlp"),
            P(None, "cfg", "mlp"),
            P(),
            P(None, "mlp", "cfg"),
            P(None, "mlp", "cfg"),
            P(),
        ),
        out_specs=(
            P(("tok", "mlp"), None, "cfg"),
            P(("tok", "mlp"), None, "cfg"),
            P("cfg", ("tok", "mlp"), None, None),
        ),
        check_vma=False,
    )
```

profile of v0, /device:TPU:1, one launch (start us, length us, event | category | flops | bytes accessed | tf_op | source)
XLA Modules:
  0.0 687.4 jit_solution(511680488462771938)
XLA Ops:
  7.2 2.5 copy.32
  10.2 295.8 %all-gather.5 = f32[128,120,4]{1,2,0:T(4,128)S(1)} all-gather(f32[1,120,4]{1,2,0:T(4,128)S(1)} %convolution_bitcast_fusion), channel_id=1, replica_groups=mesh['cfg'=2,'tok'=8,'mlp'=16] {'tok','mlp'}, dimensions={0}, use_global_device_ids=true | all-gather | bytes 247680 | tf_op jit(solution)/shard_map/all_gather | solution.py:96
  306.8 1.0 fusion.67
  309.8 0.8 fusion.84
  310.6 103.2 %all-gather.13.cloned.1.call-done = bf16[192,4,3072]{2,1,0:T(4,128)(2,1)} async-done(((bf16[12,4,3072]{2,1,0:T(4,128)(2,1)}), bf16[192,4,3072]{2,1,0:T(4,128)(2,1)}) %all-gather.13.cloned.1.call-update) | async-done | bytes 4718608 | tf_op jit(solution)/shard_map/all_gather | solution.py:106
  413.8 5.2 fusion.24
  419.7 6.6 slice.49
  426.4 7.3 %slice.50 = f32[192,4,1,64]{3,0,1,2:T(8,128)} slice(f32[192,4,1,128]{3,0,1,2:T(8,128)S(1)} %get-tuple-element.18), slice={[0:192:1], [0:4:1], [0:1:1], [1:128:2]} | slice | bytes 393216 | tf_op jit(solution)/shard_map/slice | solution.py:55
  433.7 6.6 slice.53
  440.3 7.5 %slice.54 = f32[192,4,1,64]{3,0,1,2:T(8,128)} slice(f32[192,4,1,128]{3,0,1,2:T(8,128)S(1)} %get-tuple-element.19), slice={[0:192:1], [0:4:1], [0:1:1], [1:128:2]} | slice | bytes 393216 | tf_op jit(solution)/shard_map/slice | solution.py:55
  447.9 4.1 fusion.77
  451.9 0.8 pad_maximum_fusion
  452.8 0.7 slice.80
  453.6 3.4 all-gather.2
  457.1 10.6 %fusion.14 = bf16[192,4,768]{2,0,1:T(8,128)(2,1)} fusion(bf16[1,3072,768]{2,1,0:T(8,128)(2,1)} %all-gather.21.cloned.1.call-done, bf16[192,4,3072]{2,1,0:T(4,128)(2,1)} %all-gather.13.cloned.1.call-done), kind=kOutput, calls=%fused_computation.17 | convolution fusion | flops 3629187072 | bytes 10616832 | tf_op jit(solution)/shard_map/tpd,dk->tpk/dot_general | solution.py:117
  467.7 10.2 %fusion = f32[192,4,3072]{2,0,1:T(8,128)} fusion(bf16[192,4,768]{2,0,1:T(8,128)(2,1)} %fusion.14, bf16[1,768,3072]{2,1,0:T(8,128)(2,1)} %all-gather.23.cloned.1.call-done), kind=kOutput, calls=%fused_computation.1 | convolution fusion | flops 3623878656 | bytes 15335424 | tf_op jit(solution)/shard_map/tpk,kd->tpd/dot_general | solution.py:148
  477.9 19.1 %all-gather.15.cloned.1.call-done = bf16[1536,4,1,128]{3,0,1,2:T(8,128)(2,1)} async-done(((bf16[192,4,1,128]{3,0,1,2:T(8,128)(2,1)}), bf16[1536,4,1,128]{3,0,1,2:T(8,128)(2,1)}) %all-gather.15.cloned.1.call-update) | async-done | bytes 1572880 | tf_op jit(solution)/shard_map/all_gather | solution.py:128
  497.0 4.0 fusion.92
  501.1 36.8 %all-gather.19.cloned.1.call-done = bf16[1536,4,1,1,128]{4,0,2,1,3:T(8,128)(2,1)} async-done(((bf16[192,4,1,1,128]{4,0,2,1,3:T(8,128)(2,1)}), bf16[1536,4,1,1,128]{4,0,2,1,3:T(8,128)(2,1)}) %all-gather.19.cloned.1.call-update) | async-done | bytes 1572880 | tf_op jit(solution)/shard_map/all_gather | solution.py:129
  537.9 7.8 %add_convert_fusion = bf16[192,4,3072]{2,0,1:T(8,128)(2,1)} fusion(f32[192,4,3072]{2,0,1:T(8,128)} %fusion, bf16[1536,4,1,1,128]{4,0,2,1,3:T(8,128)(2,1)} %all-gather.19.cloned.1.call-done, bf16[4,192,1536]{2,1,0:T(8,128)(2,1)} %get-tuple-element.36, bf16[1,128,3072]{2,1,0:T(8,128)(2,1)S(1)} %all-gather.2, f32[192,4]{0,1:T(4,128)S(1)} %bitcast.167), kind=kOutput, calls=%fused_computation | convolution fusion | flops 910884864 | bytes 18877440 | tf_op jit(solution)/shard_map/tpk,kd->tpd/dot_general | solution.py:147
  545.7 8.1 %copy.36 = bf16[192,4,3072]{2,1,0:T(4,128)(2,1)} copy(bf16[192,4,3072]{2,0,1:T(8,128)(2,1)} %add_convert_fusion) | data formatting | bytes 9437184 | tf_op jit(solution)/shard_map/convert_element_type | solution.py:149
  555.8 119.0 %all-reduce.3.cloned.1.call-done = bf16[192,4,3072]{2,1,0:T(4,128)(2,1)} async-done(((bf16[192,4,3072]{2,1,0:T(4,128)(2,1)}), bf16[192,4,3072]{2,1,0:T(4,128)(2,1)}) %all-reduce.3.cloned.1.call-update) | async-done | bytes 4718608
  674.8 1.3 convert_reduce_fusion
  677.1 0.7 collective-permute-start
  (67 shorter events, 7.7 us)
Async XLA Ops:
  7.2 2.7 copy-start
  7.2 2.7 copy-start.10
  7.2 299.1 %copy-start.1 = (bf16[1,12,4,3072]{3,2,1,0:T(4,128)(2,1)S(1)}, bf16[1,12,4,3072]{3,2,1,0:T(4,128)(2,1)}, u32[]{:S(2)}) copy-start(bf16[1,12,4,3072]{3,2,1,0:T(4,128)(2,1)} %param.14) | copy-start | bytes 884740
  7.2 303.4 %all-gather.17.cloned.1.call-start = ((), (), s32[]{:S(2)}) async-start(), calls=%async_computation.2 | async-start | bytes 3538944 | tf_op jit(solution)/shard_map/all_gather | solution.py:111
  9.8 404.0 %all-gather.13.cloned.1.call-start = ((), (), s32[]{:S(2)}) async-start(), calls=%async_computation | async-start | bytes 5013504 | tf_op jit(solution)/shard_map/all_gather | solution.py:106
  307.9 2.7 copy-start.7
  307.9 149.2 %all-gather.21.cloned.1.call-start = ((), (), s32[]{:S(2)}) async-start(), calls=%async_computation.4 | async-start | bytes 7077888 | tf_op jit(solution)/shard_map/all_gather | solution.py:112
  308.6 159.0 %all-gather.23.cloned.1.call-start = ((), (), s32[]{:S(2)}) async-start(), calls=%async_computation.5 | async-start | bytes 7077888 | tf_op jit(solution)/shard_map/all_gather | solution.py:144
  309.2 187.8 %all-gather.15.cloned.1.call-start = ((), (), s32[]{:S(2)}) async-start(), calls=%async_computation.1 | async-start | bytes 1769472 | tf_op jit(solution)/shard_map/all_gather | solution.py:128
  447.9 9.2 %copy-start.8 = (s32[1,4]{1,0:T(1,128)S(1)}, s32[1,4]{1,0:T(1,128)}, u32[]{:S(2)}) copy-start(s32[1,4]{1,0:T(1,128)} %param.18) | copy-start | bytes 52
  451.9 5.1 copy-start.5
  452.7 85.2 %all-gather.19.cloned.1.call-start = ((), (), s32[]{:S(2)}) async-start(), calls=%async_computation.3 | async-start | bytes 1769472 | tf_op jit(solution)/shard_map/all_gather | solution.py:129
  453.5 221.3 %all-reduce.3.cloned.1.call-start = ((), (), s32[]{:S(2)}) async-start(), calls=%async_computation.6 | async-start | bytes 9437184
  467.7 29.4 %copy-start.3 = (bf16[192,4,64]{2,0,1:T(8,128)(2,1)S(1)}, bf16[192,4,64]{2,0,1:T(8,128)(2,1)}, u32[]{:S(2)}) copy-start(bf16[192,4,64]{2,0,1:T(8,128)(2,1)} %get-tuple-element.20) | copy-start | bytes 294916
  467.7 29.4 %copy-start.4 = (bf16[192,4,64]{2,0,1:T(8,128)(2,1)S(1)}, bf16[192,4,64]{2,0,1:T(8,128)(2,1)}, u32[]{:S(2)}) copy-start(bf16[192,4,64]{2,0,1:T(8,128)(2,1)} %get-tuple-element.21) | copy-start | bytes 294916
  553.8 0.7 copy-start.11
  553.8 122.9 %copy-start.9 = (bf16[3072,64]{0,1:T(8,128)(2,1)S(1)}, bf16[3072,64]{0,1:T(8,128)(2,1)}, u32[]{:S(2)}) copy-start(bf16[3072,64]{0,1:T(8,128)(2,1)} %param.27) | copy-start | bytes 1179652
  553.8 125.4 %copy-start.6 = (f32[12,4,32]{2,1,0:T(4,128)S(1)}, f32[12,4,32]{2,1,0:T(4,128)}, u32[]{:S(2)}) copy-start(f32[12,4,32]{2,1,0:T(4,128)} %param.15) | copy-start | bytes 18436
  676.1 4.5 copy-start.2
  677.1 2.1 collective-permute-start
Sparse Core Ops, SparseCore 0:
  9.9 20.8 all-gather.16
  308.0 105.7 all-gather.12
  415.6 20.2 all-gather.20
  437.5 21.6 all-gather.22
  460.8 36.1 all-gather.14
  499.3 38.5 all-gather.18
  554.0 120.7 all-reduce.2
where the time goes:
time: 688 us; the launch traced here: 687 us
  blocking collectives  299 us (43%)
  waiting for transfers between devices  279 us (41%)
  local copies, waits for them, and re-layouts  42.4 us (6%)
  matrix products  38.4 us (6%)
  between operations  16.4 us (2%)
  other arithmetic  10.6 us (2%)
    all_gather x1, blocking collectives, on_device(): modulation = lax.all_gather(mod_part, ('tok', 'mlp'), axis=1, tiled=True)  296 us
    unnamed x8, waiting for transfers between devices  120 us
    all_gather x1, waiting for transfers between devices, on_device(): tile_input = lax.all_gather(normed, 'mlp', axis=0, tiled=True)  103 us
    all_gather x1, waiting for transfers between devices, on_device(): values_piece = lax.all_gather(values, 'tok', axis=0, tiled=True)  36.8 us
    all_gather x1, waiting for transfers between devices, on_device(): keys_piece = lax.all_gather(keys_rot, 'tok', axis=0, tiled=True)  19.1 us
    slice x2, local copies, waits for them, and re-layouts, apply_rope(): odd_part = values[..., 1::2]  14.9 us
  transfers between devices with their start and end apart: 8, of which 4 were waited for; matrix products, arithmetic and copies ran while one was open for 10% of the time, Pallas kernels for 0%

commit v1 on v0

--- a/solution.py
+++ b/solution.py
@@ -11,6 +11,16 @@
 EPSILON = 1e-06
 ROPE_BASE = 10000.0
 TIME_SHIFT = 3.0
+
+
+def recast_the_indices(incoming_x, tile_in, mesh_name):
+    return jnp.split(
+        lax.all_gather(
+            jnp.concatenate([tile_in, incoming_x], axis=1), axis_name=mesh_name, axis=0, tiled=True
+        ),
+        [tile_in.shape[1]],
+        axis=1,
+    )
 
 
 def swapped(value, axis, apart):
@@ -125,8 +135,7 @@
     ).astype(jnp.bfloat16)
     values = projected[:, :, 2].astype(jnp.bfloat16)
     activation = jax.nn.gelu(unit_pre, approximate=True).astype(jnp.bfloat16)
-    keys_piece = lax.all_gather(keys_rot, "tok", axis=0, tiled=True)
-    values_piece = lax.all_gather(values, "tok", axis=0, tiled=True)
+    keys_piece, values_piece = recast_the_indices(values, keys_rot, "tok")
     scores = jnp.einsum(
         "sphe,tphe->phst", queries, keys_piece, preferred_element_type=jnp.float32
     ) / math.sqrt(head_size)

time: 688 us -> 656 us (0.953)
  waiting for transfers between devices: 279 us -> 248 us
    all_gather x2 -> x1, waiting for transfers between devices: 55.9 us -> 28.4 us  [recast_the_indices(): lax.all_gather(jnp.concatenate([tile_in, incoming_x], axis=1), axis_name=...]
    unnamed x8 -> x7, waiting for transfers between devices: 120 us -> 117 us
  transfers between devices with their start and end apart: 8 -> 7, of which waited for: 4 -> 3; matrix products, arithmetic and copies ran while one was open for 10% -> 10% of each run, Pallas kernels for 0% -> 0%
where the time goes in v1:
time: 656 us
  blocking collectives  299 us (46%)
  waiting for transfers between devices  248 us (38%)
  local copies, waits for them, and re-layouts  41.7 us (6%)
  matrix products  38.5 us (6%)
  between operations  16.4 us (2%)
  other arithmetic  10.8 us (2%)
    all_gather x1, blocking collectives, on_device(): modulation = lax.all_gather(mod_part, ('tok', 'mlp'), axis=1, tiled=True)  296 us
    unnamed x7, waiting for transfers between devices  117 us
    all_gather x1, waiting for transfers between devices, on_device(): tile_input = lax.all_gather(normed, 'mlp', axis=0, tiled=True)  103 us
    all_gather x1, waiting for transfers between devices, recast_the_indices(): lax.all_gather(jnp.concatenate([tile_in, incoming_x], axis=1), axis_name=...  28.4 us
    slice x2, local copies, waits for them, and re-layouts, apply_rope(): even_part = values[..., 0::2]  14.7 us
    slice x2, local copies, waits for them, and re-layouts, apply_rope(): odd_part = values[..., 1::2]  13.4 us
  transfers between devices with their start and end apart: 7, of which 3 were waited for; matrix products, arithmetic and copies ran while one was open for 10% of the time, Pallas kernels for 0%

profile of v1, /device:TPU:1, one launch (start us, length us, event | category | flops | bytes accessed | tf_op | source)
XLA Modules:
  0.0 655.6 jit_solution(8687076607529613313)
XLA Ops:
  7.2 2.5 copy.34
  10.1 295.8 %all-gather.4 = f32[128,120,4]{1,2,0:T(4,128)S(1)} all-gather(f32[1,120,4]{1,2,0:T(4,128)S(1)} %convolution_bitcast_fusion), channel_id=1, replica_groups=mesh['cfg'=2,'tok'=8,'mlp'=16] {'tok','mlp'}, dimensions={0}, use_global_device_ids=true | all-gather | bytes 247680 | tf_op jit(solution)/shard_map/all_gather | solution.py:106
  306.8 1.0 fusion.55
  307.9 0.7 all-gather.17.cloned.1.call-update
  309.7 0.8 fusion.73
  310.6 103.2 %all-gather.11.cloned.1.call-done = bf16[192,4,3072]{2,1,0:T(4,128)(2,1)} async-done(((bf16[12,4,3072]{2,1,0:T(4,128)(2,1)}), bf16[192,4,3072]{2,1,0:T(4,128)(2,1)}) %all-gather.11.cloned.1.call-update) | async-done | bytes 4718608 | tf_op jit(solution)/shard_map/all_gather | solution.py:116
  413.8 5.2 fusion.22
  419.8 6.7 %slice.54 = f32[192,4,1,64]{3,0,1,2:T(8,128)S(1)} slice(f32[192,4,1,128]{3,0,1,2:T(8,128)S(1)} %get-tuple-element.33), slice={[0:192:1], [0:4:1], [0:1:1], [1:128:2]} | slice | bytes 393216 | tf_op jit(solution)/shard_map/slice | solution.py:65
  426.5 7.3 %slice.53 = f32[192,4,1,64]{3,0,1,2:T(8,128)} slice(f32[192,4,1,128]{3,0,1,2:T(8,128)S(1)} %get-tuple-element.33), slice={[0:192:1], [0:4:1], [0:1:1], [0:128:2]} | slice | bytes 393216 | tf_op jit(solution)/shard_map/slice | solution.py:64
  433.7 6.7 %slice.49 = f32[192,4,1,64]{3,0,1,2:T(8,128)S(1)} slice(f32[192,4,1,128]{3,0,1,2:T(8,128)S(1)} %get-tuple-element.34), slice={[0:192:1], [0:4:1], [0:1:1], [1:128:2]} | slice | bytes 393216 | tf_op jit(solution)/shard_map/slice | solution.py:65
  440.5 7.5 %slice.48 = f32[192,4,1,64]{3,0,1,2:T(8,128)} slice(f32[192,4,1,128]{3,0,1,2:T(8,128)S(1)} %get-tuple-element.34), slice={[0:192:1], [0:4:1], [0:1:1], [0:128:2]} | slice | bytes 393216 | tf_op jit(solution)/shard_map/slice | solution.py:64
  448.0 4.1 fusion.66
  452.1 0.9 pad_maximum_fusion
  453.0 3.2 all-gather.1
  456.4 10.6 %fusion.14 = bf16[192,4,768]{2,0,1:T(8,128)(2,1)} fusion(bf16[1,3072,768]{2,1,0:T(8,128)(2,1)} %all-gather.17.cloned.1.call-done, bf16[192,4,3072]{2,1,0:T(4,128)(2,1)} %all-gather.11.cloned.1.call-done), kind=kOutput, calls=%fused_computation.17 | convolution fusion | flops 3629187072 | bytes 10616832 | tf_op jit(solution)/shard_map/tpd,dk->tpk/dot_general | solution.py:127
  467.0 10.2 %fusion = f32[192,4,3072]{2,0,1:T(8,128)} fusion(bf16[192,4,768]{2,0,1:T(8,128)(2,1)} %fusion.14, bf16[1,768,3072]{2,1,0:T(8,128)(2,1)} %all-gather.19.cloned.1.call-done), kind=kOutput, calls=%fused_computation.1 | convolution fusion | flops 3623878656 | bytes 15335424 | tf_op jit(solution)/shard_map/tpk,kd->tpd/dot_general | solution.py:157
  477.2 28.4 %all-gather.13.cloned.1.call-done = bf16[1536,8,1,128]{3,0,1,2:T(8,128)(2,1)} async-done(((bf16[192,8,1,128]{3,0,1,2:T(8,128)(2,1)}), bf16[1536,8,1,128]{3,0,1,2:T(8,128)(2,1)}) %all-gather.13.cloned.1.call-update) | async-done | bytes 3145744 | tf_op jit(solution)/shard_map/all_gather | solution.py:18
  505.6 4.1 fusion.81
  509.7 7.8 %add_convert_fusion = bf16[192,4,3072]{2,0,1:T(8,128)(2,1)} fusion(f32[192,4,3072]{2,0,1:T(8,128)} %fusion, bf16[1536,8,1,128]{3,0,1,2:T(8,128)(2,1)} %all-gather.13.cloned.1.call-done, bf16[4,192,1536]{2,1,0:T(8,128)(2,1)} %get-tuple-element.32, bf16[1,128,3072]{2,1,0:T(8,128)(2,1)S(1)} %all-gather.1, f32[192,4]{0,1:T(4,128)S(1)} %bitcast.167), kind=kOutput, calls=%fused_computation | convolution fusion | flops 910884864 | bytes 18877440 | tf_op jit(solution)/shard_map/tpk,kd->tpd/dot_general | solution.py:156
  517.5 8.1 %copy.39 = bf16[192,4,3072]{2,1,0:T(4,128)(2,1)} copy(bf16[192,4,3072]{2,0,1:T(8,128)(2,1)} %add_convert_fusion) | data formatting | bytes 9437184 | tf_op jit(solution)/shard_map/convert_element_type | solution.py:158
  525.6 0.6 copy-done.12
  527.6 115.4 %all-reduce.3.cloned.1.call-done = bf16[192,4,3072]{2,1,0:T(4,128)(2,1)} async-done(((bf16[192,4,3072]{2,1,0:T(4,128)(2,1)}), bf16[192,4,3072]{2,1,0:T(4,128)(2,1)}) %all-reduce.3.cloned.1.call-update) | async-done | bytes 4718608
  643.0 1.3 convert_reduce_fusion
  645.3 0.7 collective-permute-start
  (68 shorter events, 6.5 us)
Async XLA Ops:
  7.2 2.6 copy-start
  7.2 2.6 copy-start.11
  7.2 299.0 %copy-start.1 = (bf16[1,12,4,3072]{3,2,1,0:T(4,128)(2,1)S(1)}, bf16[1,12,4,3072]{3,2,1,0:T(4,128)(2,1)}, u32[]{:S(2)}) copy-start(bf16[1,12,4,3072]{3,2,1,0:T(4,128)(2,1)} %param.14) | copy-start | bytes 884740
  7.2 303.4 %all-gather.15.cloned.1.call-start = ((), (), s32[]{:S(2)}) async-start(), calls=%async_computation.2 | async-start | bytes 3538944 | tf_op jit(solution)/shard_map/all_gather | solution.py:121
  9.8 404.0 %all-gather.11.cloned.1.call-start = ((), (), s32[]{:S(2)}) async-start(), calls=%async_computation | async-start | bytes 5013504 | tf_op jit(solution)/shard_map/all_gather | solution.py:116
  307.8 2.7 copy-start.8
  307.9 148.5 %all-gather.17.cloned.1.call-start = ((), (), s32[]{:S(2)}) async-start(), calls=%async_computation.3 | async-start | bytes 7077888 | tf_op jit(solution)/shard_map/all_gather | solution.py:122
  308.6 158.4 %all-gather.19.cloned.1.call-start = ((), (), s32[]{:S(2)}) async-start(), calls=%async_computation.4 | async-start | bytes 7077888 | tf_op jit(solution)/shard_map/all_gather | solution.py:153
  309.2 196.4 %all-gather.13.cloned.1.call-start = ((), (), s32[]{:S(2)}) async-start(), calls=%async_computation.1 | async-start | bytes 3538944 | tf_op jit(solution)/shard_map/all_gather | solution.py:18
  448.0 5.1 copy-start.3
  448.0 8.3 %copy-start.9 = (s32[1,4]{1,0:T(1,128)S(1)}, s32[1,4]{1,0:T(1,128)}, u32[]{:S(2)}) copy-start(s32[1,4]{1,0:T(1,128)} %param.18) | copy-start | bytes 52
  452.1 4.2 copy-start.6
  453.0 190.0 %all-reduce.3.cloned.1.call-start = ((), (), s32[]{:S(2)}) async-start(), calls=%async_computation.5 | async-start | bytes 9437184
  467.0 38.6 %copy-start.4 = (bf16[192,4,64]{2,0,1:T(8,128)(2,1)S(1)}, bf16[192,4,64]{2,0,1:T(8,128)(2,1)}, u32[]{:S(2)}) copy-start(bf16[192,4,64]{2,0,1:T(8,128)(2,1)} %get-tuple-element.16) | copy-start | bytes 294916
  467.0 38.6 %copy-start.5 = (bf16[192,4,64]{2,0,1:T(8,128)(2,1)S(1)}, bf16[192,4,64]{2,0,1:T(8,128)(2,1)}, u32[]{:S(2)}) copy-start(bf16[192,4,64]{2,0,1:T(8,128)(2,1)} %get-tuple-element.17) | copy-start | bytes 294916
  525.6 0.7 copy-start.12
  525.6 119.4 %copy-start.10 = (bf16[3072,64]{0,1:T(8,128)(2,1)S(1)}, bf16[3072,64]{0,1:T(8,128)(2,1)}, u32[]{:S(2)}) copy-start(bf16[3072,64]{0,1:T(8,128)(2,1)} %param.27) | copy-start | bytes 1179652
  525.6 121.8 %copy-start.7 = (f32[12,4,32]{2,1,0:T(4,128)S(1)}, f32[12,4,32]{2,1,0:T(4,128)}, u32[]{:S(2)}) copy-start(f32[12,4,32]{2,1,0:T(4,128)} %param.15) | copy-start | bytes 18436
  644.3 4.5 copy-start.2
  645.3 2.1 collective-permute-start
Sparse Core Ops, SparseCore 0:
  9.9 20.8 all-gather.14
  308.0 105.7 all-gather.10
  415.6 20.2 all-gather.16
  437.5 21.1 all-gather.18
  460.4 45.1 all-gather.12
  525.7 117.2 all-reduce.2
